TPU v7x, 256 devices: a whole 4x4x8 slice. The times are simulated.
256 devices in a mesh: pipe: 4 (over x), seq: 64 (over y, z, core).
Axes of the slice: x: 4, y: 4, z: 8, core: 2. Of those that a mesh axis runs over, the one named last changes fastest.
Arguments:
- arriving: bfloat16 [4, 65536, 2048], P('pipe', 'seq'), may hold values from -6 to 6
- loss_grad: bfloat16 [65536, 2048], P('seq', 'pipe'), may hold values from -6 to 6
- first_blocks: bfloat16 [4, 256, 256, 256], P('pipe', 'seq'), may hold values from -0.375 to 0.375
- second_blocks: bfloat16 [4, 256, 256, 256], P('pipe', 'seq'), may hold values from -0.375 to 0.375
- inner_gain: bfloat16 [4, 2048], P('pipe'), may hold values from 0.25 to 1.75
- outer_gain: bfloat16 [4, 2048], P('pipe'), may hold values from 0.25 to 1.75
Outputs:
- entering: bfloat16 [4, 65536, 2048], P('pipe', 'seq')
- leaving: bfloat16 [65536, 2048], P('seq', 'pipe')
All inputs are finite; a program needn't handle non-finite values.
Results may differ from a plain program's by a relative error of at most 0.0059.
Values may be sent and summed in bfloat16 or wider, within the bound.
No kernel may reach another device: no remote copies, remote signals or barrier semaphores. Data moves between devices by JAX's collectives and lax.ppermute only.
A program may use at most 128 MiB of HBM per device.

v0:
```python
import jax
import jax.numpy as jnp
from jax import lax
from jax.sharding import PartitionSpec as P


def shifted(block, axis, distance):
    devices = range(lax.axis_size(axis))
    route = [((i - distance) % len(devices), i) for i in devices]
    return lax.ppermute(block, axis, route)


def from_root(array, axis, root):
    mine = lax.axis_index(axis) == root
    return lax.psum(jnp.where(mine, array, jnp.zeros_like(array)), axis)


def mixer(gradient, first_part, second_part, inner_part, outer_part):
    row_count = first_part.shape[0]
    block_order = first_part.shape[1]
    blocked = gradient.reshape(row_count, block_order, gradient.shape[1]).astype(jnp.float32)
    scaled = (blocked * inner_part.astype(jnp.float32)).astype(jnp.bfloat16)
    mixed = jnp.einsum(
        "kjc,jki->ijc",
        lax.all_to_all(scaled, "seq", split_axis=1, concat_axis=0, tiled=True),
        second_part,
        preferred_element_type=jnp.float32,
    ).astype(jnp.bfloat16)
    returned = lax.all_to_all(mixed, "seq", split_axis=0, concat_axis=1, tiled=True)
    spread = jnp.einsum("ikc,ikj->ijc", returned, first_part, preferred_element_type=jnp.float32)
    result = blocked + outer_part.astype(jnp.float32) * spread
    return result.astype(jnp.bfloat16).reshape(gradient.shape)


def per_device(arriving, loss_grad, first_blocks, second_blocks, inner_gain, outer_gain):
    sections = lax.axis_size("pipe")
    position = lax.axis_index("pipe")
    whole_loss = lax.all_gather(loss_grad, "pipe", axis=1, tiled=True)
    own_result = mixer(arriving[0], first_blocks[0], second_blocks[0], inner_gain[0], outer_gain[0])
    passed = shifted(own_result, "pipe", -1)
    exit_root = sections - 1
    source = jnp.where(position == sections - 1, whole_loss, passed)
    entering = mixer(source, first_blocks[0], second_blocks[0], inner_gain[0], outer_gain[0])
    copied = from_root(passed, "pipe", exit_root)
    channel_width = loss_grad.shape[1]
    leaving = lax.dynamic_slice_in_dim(copied, position * channel_width, channel_width, 1)
    return (entering[None], leaving)


def solution(mesh):
    placed = (
        P("pipe", "seq", None),
        P("seq", "pipe"),
        P("pipe", "seq", None, None),
        P("pipe", "seq", None, None),
        P("pipe", None),
        P("pipe", None),
    )
    return jax.shard_map(
        per_device,
        mesh=mesh,
        in_specs=placed,
        out_specs=(P("pipe", "seq", None), P("seq", "pipe")),
        check_vma=False,
    )
```

profile of v0, /device:TPU:1, one launch (start us, length us, event | category | flops | bytes accessed | tf_op | source)
XLA Modules:
  0.0 639.2 jit_solution(10214228244827802752)
XLA Ops:
  7.9 3.3 fusion
  11.2 3.2 copy.24
  14.5 109.1 %all_to_all.72 = bf16[4,256,2048]{2,0,1:T(4,128)(2,1)S(1)} all-to-all(bf16[4,256,2048]{2,0,1:T(4,128)(2,1)S(1)} %copy.24), channel_id=1, replica_groups=mesh['pipe'=4,'seq'=64] {'seq'}, dimensions={1} | all-to-all | bytes 8388608 | tf_op jit(solution)/shard_map/all_to_all | solution.py:25
  123.6 8.3 %copy.25 = bf16[4,64,4,2048]{3,2,0,1:T(4,128)(2,1)S(1)} copy(bf16[4,64,4,2048]{3,0,2,1:T(4,128)(2,1)S(1)} %bitcast.44) | data formatting | bytes 8388608 | tf_op jit(solution)/shard_map/all_to_all | solution.py:25
  131.9 7.7 %convert_bitcast_fusion.1 = bf16[256,4,2048]{0,2,1:T(8,128)(2,1)} fusion(bf16[256,4,2048]{2,1,0:T(4,128)(2,1)S(1)} %bitcast.45, bf16[1,4,256,256]{3,2,1,0:T(8,128)(2,1)S(1)} %copy-done), kind=kOutput, calls=%fused_computation.13 | convolution fusion | flops 1075838976 | bytes 8912896 | tf_op jit(solution)/shard_map/kjc,jki->ijc/dot_general | solution.py:23
  139.6 7.9 %copy.27 = bf16[256,4,2048]{2,1,0:T(4,128)(2,1)} copy(bf16[256,4,2048]{0,2,1:T(8,128)(2,1)} %convert_bitcast_fusion.1) | data formatting | bytes 8388608 | tf_op jit(solution)/shard_map/convert_element_type | solution.py:28
  147.5 6.2 all-to-all-start.1
  154.4 95.1 %all-to-all-done.1 = bf16[256,4,2048]{2,1,0:T(4,128)(2,1)} async-done(((bf16[256,4,2048]{2,1,0:T(4,128)(2,1)}), bf16[256,4,2048]{2,1,0:T(4,128)(2,1)}, u32[]{:S(2)}, u32[]{:S(2)}) %all-to-all-start.1) | async-done | bytes 4194336 | tf_op jit(solution)/shard_map/all_to_all | solution.py:29
  249.5 7.0 %copy.28 = bf16[4,64,4,2048]{3,2,1,0:T(4,128)(2,1)} copy(bf16[4,64,4,2048]{3,2,0,1:T(4,128)(2,1)} %bitcast.10) | data formatting | bytes 8388608 | tf_op jit(solution)/shard_map/all_to_all | solution.py:29
  256.5 7.0 %all_to_all.59 = bf16[4,256,2048]{2,1,0:T(8,128)(2,1)} reshape(bf16[4,64,4,2048]{3,2,1,0:T(4,128)(2,1)} %copy.28) | data formatting | bytes 8388608 | tf_op jit(solution)/shard_map/all_to_all | solution.py:29
  263.5 6.9 %fusion.1 = bf16[4,256,2048]{2,1,0:T(8,128)(2,1)} fusion(bf16[4,256,2048]{2,1,0:T(8,128)(2,1)} %bitcast.49, bf16[4,256,2048]{2,1,0:T(8,128)(2,1)} %all_to_all.59, f32[2048]{0:T(1024)S(1)} %bitcast.53, bf16[1,4,256,256]{3,2,1,0:T(8,128)(2,1)S(1)} %copy-done.2), kind=kOutput, calls=%fused_computation.5 | convolution fusion | flops 1082130432 | bytes 13115392 | tf_op jit(solution)/shard_map/ikc,ikj->ijc/dot_general | solution.py:30
  270.5 2.5 collective-permute-start
  273.0 90.0 %collective-permute-done = bf16[1024,2048]{1,0:T(8,128)(2,1)} collective-permute-done((bf16[1024,2048]{1,0:T(8,128)(2,1)}, bf16[1024,2048]{1,0:T(8,128)(2,1)}, u32[]{:S(2)}, u32[]{:S(2)}) %collective-permute-start) | collective-permute-done | bytes 4194336 | tf_op jit(solution)/shard_map/ppermute | solution.py:10
  362.9 3.9 broadcast_select_fusion
  369.9 3.2 copy.30
  373.2 101.9 %all_to_all.73 = bf16[4,256,2048]{2,0,1:T(4,128)(2,1)S(1)} all-to-all(bf16[4,256,2048]{2,0,1:T(4,128)(2,1)S(1)} %copy.30), channel_id=1, replica_groups=mesh['pipe'=4,'seq'=64] {'seq'}, dimensions={1} | all-to-all | bytes 8388608 | tf_op jit(solution)/shard_map/all_to_all | solution.py:25
  475.1 8.3 %copy.31 = bf16[4,64,4,2048]{3,2,0,1:T(4,128)(2,1)S(1)} copy(bf16[4,64,4,2048]{3,0,2,1:T(4,128)(2,1)S(1)} %bitcast.46) | data formatting | bytes 8388608 | tf_op jit(solution)/shard_map/all_to_all | solution.py:25
  483.4 7.5 %convert_bitcast_fusion = bf16[256,4,2048]{0,2,1:T(8,128)(2,1)} fusion(bf16[256,4,2048]{2,1,0:T(4,128)(2,1)S(1)} %bitcast.47, bf16[1,4,256,256]{3,2,1,0:T(8,128)(2,1)S(1)} %copy-done), kind=kOutput, calls=%fused_computation.12 | convolution fusion | flops 1075838976 | bytes 8912896 | tf_op jit(solution)/shard_map/kjc,jki->ijc/dot_general | solution.py:23
  490.8 8.0 %copy.33 = bf16[256,4,2048]{2,1,0:T(4,128)(2,1)} copy(bf16[256,4,2048]{0,2,1:T(8,128)(2,1)} %convert_bitcast_fusion) | data formatting | bytes 8388608 | tf_op jit(solution)/shard_map/convert_element_type | solution.py:28
  498.8 6.0 all-to-all-start.3
  505.6 103.4 %all-reduce.2.cloned.1.call-done = bf16[1024,2048]{1,0:T(8,128)(2,1)} async-done(((bf16[1024,2048]{1,0:T(8,128)(2,1)}), bf16[1024,2048]{1,0:T(8,128)(2,1)}) %all-reduce.2.cloned.1.call-update) | async-done | bytes 4194320 | tf_op jit(solution)/shard_map/psum | solution.py:15
  611.2 7.0 %copy.34 = bf16[4,64,4,2048]{3,2,1,0:T(4,128)(2,1)} copy(bf16[4,64,4,2048]{3,2,0,1:T(4,128)(2,1)} %bitcast.21) | data formatting | bytes 8388608 | tf_op jit(solution)/shard_map/all_to_all | solution.py:29
  618.2 6.9 %all_to_all.67 = bf16[4,256,2048]{2,1,0:T(8,128)(2,1)} reshape(bf16[4,64,4,2048]{3,2,1,0:T(4,128)(2,1)} %copy.34) | data formatting | bytes 8388608 | tf_op jit(solution)/shard_map/all_to_all | solution.py:29
  625.2 6.9 %fusion.3 = bf16[4,256,2048]{2,1,0:T(8,128)(2,1)} fusion(bf16[4,256,2048]{2,1,0:T(8,128)(2,1)} %bitcast.43, bf16[4,256,2048]{2,1,0:T(8,128)(2,1)} %all_to_all.67, f32[2048]{0:T(1024)S(1)} %bitcast.54, bf16[1,4,256,256]{3,2,1,0:T(8,128)(2,1)S(1)} %copy-done.2), kind=kOutput, calls=%fused_computation.7 | convolution fusion | flops 1082130432 | bytes 13115392 | tf_op jit(solution)/shard_map/ikc,ikj->ijc/dot_general | solution.py:30
  (18 shorter events, 7.6 us)
Async XLA Ops:
  7.2 124.7 %copy-start = (bf16[1,4,256,256]{3,2,1,0:T(8,128)(2,1)S(1)}, bf16[1,4,256,256]{3,2,1,0:T(8,128)(2,1)}, u32[]{:S(2)}) copy-start(bf16[1,4,256,256]{3,2,1,0:T(8,128)(2,1)} %param.9) | copy-start | bytes 1572868
  147.5 6.9 %copy-start.3 = (bf16[1,2048]{1,0:T(2,128)(2,1)S(1)}, bf16[1,2048]{1,0:T(2,128)(2,1)}, u32[]{:S(2)}) copy-start(bf16[1,2048]{1,0:T(2,128)(2,1)} %param.11) | copy-start | bytes 12292
  147.5 102.0 %all-to-all-start.1 = ((bf16[256,4,2048]{2,1,0:T(4,128)(2,1)}), bf16[256,4,2048]{2,1,0:T(4,128)(2,1)}, u32[]{:S(2)}, u32[]{:S(2)}) async-start(bf16[256,4,2048]{2,1,0:T(4,128)(2,1)} %copy.27), calls=%async_computation.1 | async-start | bytes 8388608 | tf_op jit(solution)/shard_map/all_to_all | solution.py:29
  153.7 119.3 %all-gather.2.cloned.1.call-start = ((), (), s32[]{:S(2)}) async-start(), calls=%async_computation.4 | async-start | bytes 5242880 | tf_op jit(solution)/shard_map/all_gather | solution.py:38
  256.5 7.0 %copy-start.2 = (bf16[1,4,256,256]{3,2,1,0:T(8,128)(2,1)S(1)}, bf16[1,4,256,256]{3,2,1,0:T(8,128)(2,1)}, u32[]{:S(2)}) copy-start(bf16[1,4,256,256]{3,2,1,0:T(8,128)(2,1)} %param.8) | copy-start | bytes 1572868
  270.5 92.5 %collective-permute-start = (bf16[1024,2048]{1,0:T(8,128)(2,1)}, bf16[1024,2048]{1,0:T(8,128)(2,1)}, u32[]{:S(2)}, u32[]{:S(2)}) collective-permute-start(bf16[1024,2048]{1,0:T(8,128)(2,1)} %bitcast.13), channel_id=1, source_target_pairs={{64,0},{128,64},{192,128},{0,192},{65,1},{129,65},{193,129},{1,193... | collective-permute-start | bytes 12582920 | tf_op jit(solution)/shard_map/ppermute | solution.py:10
  366.8 1.9 copy-start.1
  498.8 112.4 %all-to-all-start.3 = ((bf16[256,4,2048]{2,1,0:T(4,128)(2,1)}), bf16[256,4,2048]{2,1,0:T(4,128)(2,1)}, u32[]{:S(2)}, u32[]{:S(2)}) async-start(bf16[256,4,2048]{2,1,0:T(4,128)(2,1)} %copy.33), calls=%async_computation.3 | async-start | bytes 8388608 | tf_op jit(solution)/shard_map/all_to_all | solution.py:29
  504.8 104.1 %all-reduce.2.cloned.1.call-start = ((), (), s32[]{:S(2)}) async-start(), calls=%async_computation.5 | async-start | bytes 8388608 | tf_op jit(solution)/shard_map/psum | solution.py:15
Sparse Core Ops, SparseCore 0:
  156.3 51.5 all-gather.1
  508.6 100.3 all-reduce.1
where the time goes:
time: 645 us; the launch traced here: 639 us
  waiting for transfers between devices  290 us (45%)
  blocking collectives  211 us (33%)
  local copies, waits for them, and re-layouts  71.2 us (11%)
  matrix products  29 us (4%)
  starting transfers between devices  14.7 us (2%)
  between operations  14.4 us (2%)
  other arithmetic  9.1 us (1%)
    all_to_all x2, blocking collectives, mixer(): lax.all_to_all(scaled, 'seq', split_axis=1, concat_axis=0, tiled=True)  211 us
    psum x1, waiting for transfers between devices, from_root(): return lax.psum(jnp.where(mine, array, jnp.zeros_like(array)), axis)  103 us
    all_to_all x2, waiting for transfers between devices, mixer(): lax.all_to_all(mixed, 'seq', split_axis=0, concat_axis=1, tiled=True)  95.1 us
    ppermute x1, waiting for transfers between devices, shifted(): return lax.ppermute(block, axis, route)  90 us
    all_to_all x4, local copies, waits for them, and re-layouts, mixer(): lax.all_to_all(mixed, 'seq', split_axis=0, concat_axis=1, tiled=True)  27.9 us
    all_to_all x2, local copies, waits for them, and re-layouts, mixer(): lax.all_to_all(scaled, 'seq', split_axis=1, concat_axis=0, tiled=True)  16.6 us
    convert_element_type x2, local copies, waits for them, and re-layouts, mixer(): mixed = jnp.einsum('kjc,jki->ijc', lax.all_to_all(scaled, 'seq', split_ax...  15.9 us
    dot_general x2, matrix products, mixer(): jnp.einsum('kjc,jki->ijc', lax.all_to_all(scaled, 'seq', split_axis=1, co...  15.2 us
  transfers between devices with their start and end apart: 5, of which 3 were waited for; matrix products, arithmetic and copies ran while one was open for 3% of the time, Pallas kernels for 0%

commit v1 on v0

--- a/solution.py
+++ b/solution.py
@@ -26,7 +26,10 @@
         second_part,
         preferred_element_type=jnp.float32,
     ).astype(jnp.bfloat16)
-    returned = lax.all_to_all(mixed, "seq", split_axis=0, concat_axis=1, tiled=True)
+    returned = jnp.concatenate(
+        lax.all_to_all(jnp.stack(jnp.split(mixed, lax.axis_size("seq"), axis=0)), "seq", 0, 0),
+        axis=1,
+    )
     spread = jnp.einsum("ikc,ikj->ijc", returned, first_part, preferred_element_type=jnp.float32)
     result = blocked + outer_part.astype(jnp.float32) * spread
     return result.astype(jnp.bfloat16).reshape(gradient.shape)

time: 645 us -> 693 us (1.074)
  local copies, waits for them, and re-layouts: 71.2 us -> 116 us
    unnamed x8 -> x134, local copies, waits for them, and re-layouts: 1.96 us -> 84.1 us
    all_to_all x4 -> x0, local copies, waits for them, and re-layouts: 27.9 us -> none  [mixer(): lax.all_to_all(mixed, 'seq', split_axis=0, concat_axis=1, tiled=True)]
    convert_element_type x2 -> x0, local copies, waits for them, and re-layouts: 15.9 us -> none  [mixer(): mixed = jnp.einsum('kjc,jki->ijc', lax.all_to_all(scaled, 'seq', split_ax...]
    dot_general x2, matrix products: 15.2 us -> 6.96 us  [mixer(): jnp.einsum('kjc,jki->ijc', lax.all_to_all(scaled, 'seq', split_axis=1, co...]
    dot_general x2, matrix products: 13.9 us -> 21.7 us  [mixer(): jnp.einsum('ikc,ikj->ijc', returned, first_part, preferred_element_type=j...]
    all_to_all x2 -> x4, local copies, waits for them, and re-layouts: 16.6 us -> 21.9 us  [mixer(): lax.all_to_all(scaled, 'seq', split_axis=1, concat_axis=0, tiled=True)]
  transfers between devices with their start and end apart: 5 -> 5, of which waited for: 3 -> 3; matrix products, arithmetic and copies ran while one was open for 3% -> 2% of each run, Pallas kernels for 0% -> 0%
where the time goes in v1:
time: 693 us; the launch traced here: 684 us
  waiting for transfers between devices  290 us (42%)
  blocking collectives  211 us (30%)
  local copies, waits for them, and re-layouts  116 us (17%)
  matrix products  28.7 us (4%)
  starting transfers between devices  14.9 us (2%)
  between operations  14.4 us (2%)
  other arithmetic  9.1 us (1%)
    all_to_all x2, blocking collectives, mixer(): lax.all_to_all(scaled, 'seq', split_axis=1, concat_axis=0, tiled=True)  211 us
    psum x1, waiting for transfers between devices, from_root(): return lax.psum(jnp.where(mine, array, jnp.zeros_like(array)), axis)  103 us
    all_to_all x2, waiting for transfers between devices, mixer(): lax.all_to_all(jnp.stack(jnp.split(mixed, lax.axis_size('seq'), axis=0)),...  95.1 us
    ppermute x1, waiting for transfers between devices, shifted(): return lax.ppermute(block, axis, route)  90 us
    unnamed x134, local copies, waits for them, and re-layouts  84.1 us
    all_to_all x4, local copies, waits for them, and re-layouts, mixer(): lax.all_to_all(scaled, 'seq', split_axis=1, concat_axis=0, tiled=True)  21.9 us
    dot_general x2, matrix products, mixer(): jnp.einsum('ikc,ikj->ijc', returned, first_part, preferred_element_type=j...  21.7 us
  transfers between devices with their start and end apart: 5, of which 3 were waited for; matrix products, arithmetic and copies ran while one was open for 2% of the time, Pallas kernels for 0%

profile of v1, /device:TPU:1, one launch (start us, length us, event | category | flops | bytes accessed | tf_op | source)
XLA Modules:
  0.0 683.8 jit_solution(12270135655021012857)
XLA Ops:
  7.2 0.8 convert_element_type.76
  7.9 3.3 fusion
  11.2 3.2 copy.16
  14.5 109.1 %all_to_all.46 = bf16[4,256,2048]{2,0,1:T(4,128)(2,1)S(1)} all-to-all(bf16[4,256,2048]{2,0,1:T(4,128)(2,1)S(1)} %copy.16), channel_id=1, replica_groups=mesh['pipe'=4,'seq'=64] {'seq'}, dimensions={1} | all-to-all | bytes 8388608 | tf_op jit(solution)/shard_map/all_to_all | solution.py:25
  123.6 4.1 copy.37
  127.7 6.9 %all_to_all.35 = bf16[256,4,2048]{2,0,1:T(8,128)(2,1)} reshape(bf16[64,4,4,2048]{3,1,0,2:T(4,128)(2,1)} %bitcast.561) | data formatting | bytes 8388608 | tf_op jit(solution)/shard_map/all_to_all | solution.py:25
  134.6 3.5 convert_bitcast_fusion.1
  180.1 6.2 all-to-all-start.1
  187.0 95.1 %all-to-all-done.1 = bf16[64,4,4,2048]{3,1,2,0:T(4,128)(2,1)} async-done(((bf16[64,4,4,2048]{3,1,2,0:T(4,128)(2,1)}), bf16[64,4,4,2048]{3,1,2,0:T(4,128)(2,1)}, u32[]{:S(2)}, u32[]{:S(2)}) %all-to-all-start.1) | async-done | bytes 4194336 | tf_op jit(solution)/shard_map/all_to_all | solution.py:30
  282.1 10.9 %fusion.1 = bf16[4,256,2048]{2,1,0:T(8,128)(2,1)} fusion(bf16[4,256,2048]{2,1,0:T(8,128)(2,1)} %bitcast.565, bf16[4,256,2048]{2,0,1:T(4,128)(2,1)} %bitcast.73, f32[2048]{0:T(1024)S(1)} %bitcast.568, bf16[1,4,256,256]{3,2,1,0:T(8,128)(2,1)S(1)} %copy-done.3), kind=kOutput, calls=%fused_computation.5 | convolution fusion | flops 1082130432 | bytes 13115392 | tf_op jit(solution)/shard_map/ikc,ikj->ijc/dot_general | solution.py:33
  293.0 2.5 collective-permute-start
  295.5 90.0 %collective-permute-done = bf16[1024,2048]{1,0:T(8,128)(2,1)} collective-permute-done((bf16[1024,2048]{1,0:T(8,128)(2,1)}, bf16[1024,2048]{1,0:T(8,128)(2,1)}, u32[]{:S(2)}, u32[]{:S(2)}) %collective-permute-start) | collective-permute-done | bytes 4194336 | tf_op jit(solution)/shard_map/ppermute | solution.py:10
  385.5 3.9 broadcast_select_fusion
  389.4 1.9 copy-done.1
  391.3 1.2 fusion.2
  392.5 3.2 copy.21
  395.7 101.9 %all_to_all.47 = bf16[4,256,2048]{2,0,1:T(4,128)(2,1)S(1)} all-to-all(bf16[4,256,2048]{2,0,1:T(4,128)(2,1)S(1)} %copy.21), channel_id=1, replica_groups=mesh['pipe'=4,'seq'=64] {'seq'}, dimensions={1} | all-to-all | bytes 8388608 | tf_op jit(solution)/shard_map/all_to_all | solution.py:25
  497.6 4.1 copy.36
  501.6 6.9 %all_to_all.40 = bf16[256,4,2048]{2,0,1:T(8,128)(2,1)} reshape(bf16[64,4,4,2048]{3,1,0,2:T(4,128)(2,1)} %bitcast.563) | data formatting | bytes 8388608 | tf_op jit(solution)/shard_map/all_to_all | solution.py:25
  508.5 3.5 convert_bitcast_fusion
  553.4 6.0 all-to-all-start.3
  560.2 103.4 %all-reduce.2.cloned.1.call-done = bf16[1024,2048]{1,0:T(8,128)(2,1)} async-done(((bf16[1024,2048]{1,0:T(8,128)(2,1)}), bf16[1024,2048]{1,0:T(8,128)(2,1)}) %all-reduce.2.cloned.1.call-update) | async-done | bytes 4194320 | tf_op jit(solution)/shard_map/psum | solution.py:15
  663.6 2.3 constant_dynamic-slice_fusion
  665.9 10.9 %fusion.3 = bf16[4,256,2048]{2,1,0:T(8,128)(2,1)} fusion(bf16[4,256,2048]{2,1,0:T(8,128)(2,1)} %bitcast.559, bf16[4,256,2048]{2,0,1:T(4,128)(2,1)} %bitcast.147, f32[2048]{0:T(1024)S(1)} %bitcast.569, bf16[1,4,256,256]{3,2,1,0:T(8,128)(2,1)S(1)} %copy-done.3), kind=kOutput, calls=%fused_computation.7 | convolution fusion | flops 1082130432 | bytes 13115392 | tf_op jit(solution)/shard_map/ikc,ikj->ijc/dot_general | solution.py:33
  (142 shorter events, 85.0 us)
Async XLA Ops:
  7.2 127.4 %copy-start = (bf16[1,4,256,256]{3,2,1,0:T(8,128)(2,1)S(1)}, bf16[1,4,256,256]{3,2,1,0:T(8,128)(2,1)}, u32[]{:S(2)}) copy-start(bf16[1,4,256,256]{3,2,1,0:T(8,128)(2,1)} %param.9) | copy-start | bytes 1572868
  180.1 6.9 %copy-start.2 = (bf16[1,2048]{1,0:T(2,128)(2,1)S(1)}, bf16[1,2048]{1,0:T(2,128)(2,1)}, u32[]{:S(2)}) copy-start(bf16[1,2048]{1,0:T(2,128)(2,1)} %param.11) | copy-start | bytes 12292
  180.1 102.0 %copy-start.3 = (bf16[1,4,256,256]{3,2,1,0:T(8,128)(2,1)S(1)}, bf16[1,4,256,256]{3,2,1,0:T(8,128)(2,1)}, u32[]{:S(2)}) copy-start(bf16[1,4,256,256]{3,2,1,0:T(8,128)(2,1)} %param.8) | copy-start | bytes 1572868
  180.1 102.0 %all-to-all-start.1 = ((bf16[64,4,4,2048]{3,1,2,0:T(4,128)(2,1)}), bf16[64,4,4,2048]{3,1,2,0:T(4,128)(2,1)}, u32[]{:S(2)}, u32[]{:S(2)}) async-start(bf16[64,4,4,2048]{3,1,2,0:T(4,128)(2,1)} %constant_dynamic-update-slice_fusion), calls=%async_computation.1 | async-start | bytes 8388608 | tf_op jit(solution)/shard_map/all_to_all | solution.py:30
  186.3 109.2 %all-gather.2.cloned.1.call-start = ((), (), s32[]{:S(2)}) async-start(), calls=%async_computation.4 | async-start | bytes 5242880 | tf_op jit(solution)/shard_map/all_gather | solution.py:41
  293.0 92.5 %collective-permute-start = (bf16[1024,2048]{1,0:T(8,128)(2,1)}, bf16[1024,2048]{1,0:T(8,128)(2,1)}, u32[]{:S(2)}, u32[]{:S(2)}) collective-permute-start(bf16[1024,2048]{1,0:T(8,128)(2,1)} %bitcast.76), channel_id=1, source_target_pairs={{64,0},{128,64},{192,128},{0,192},{65,1},{129,65},{193,129},{1,193... | collective-permute-start | bytes 12582920 | tf_op jit(solution)/shard_map/ppermute | solution.py:10
  389.4 1.9 copy-start.1
  553.4 112.4 %all-to-all-start.3 = ((bf16[64,4,4,2048]{3,1,2,0:T(4,128)(2,1)}), bf16[64,4,4,2048]{3,1,2,0:T(4,128)(2,1)}, u32[]{:S(2)}, u32[]{:S(2)}) async-start(bf16[64,4,4,2048]{3,1,2,0:T(4,128)(2,1)} %constant_dynamic-update-slice_fusion.64), calls=%async_computation.3 | async-start | bytes 8388608 | tf_op jit(solution)/shard_map/all_to_all | solution.py:30
  559.5 104.1 %all-reduce.2.cloned.1.call-start = ((), (), s32[]{:S(2)}) async-start(), calls=%async_computation.5 | async-start | bytes 8388608 | tf_op jit(solution)/shard_map/psum | solution.py:15
Sparse Core Ops, SparseCore 0:
  188.9 51.5 all-gather.1
  563.2 100.3 all-reduce.1
